TPU v7x, 256 devices: a whole 4x4x8 slice. The times are simulated.
256 devices in a mesh: seq: 16 (over z_lo, x), hid: 16 (over z_hi, y, core).
Axes of the slice: x: 4, y: 4, z: 8 (z_hi: 2, z_lo: 4; z = z_hi * 4 + z_lo), core: 2. Of those that a mesh axis runs over, the one named last changes fastest.
Arguments:
- tokens: bfloat16 [65536, 2048], P('seq', 'hid'), may hold values from -6 to 6
- cotangent: bfloat16 [65536, 2048], P('seq', 'hid'), may hold values from -6 to 6
- seq_first: bfloat16 [128, 512, 512], P('seq'), may hold values from -0.25 to 0.25
- seq_second: bfloat16 [512, 128, 128], P('seq'), may hold values from -0.5 to 0.5
- feat_first: bfloat16 [32, 64, 64], P('hid'), may hold values from -0.75 to 0.75
- feature_second_blocks: bfloat16 [64, 32, 32], P('hid'), may hold values from -1 to 1
- gate_scale: float32 [2048], P('hid'), may hold values from 0.5 to 2
- gate_bias: float32 [2048], P('hid'), may hold values from -3 to 3
Outputs:
- result: bfloat16 [65536, 2048], P('seq', 'hid')
- token_grad: bfloat16 [65536, 2048], P('seq', 'hid')
- first_grad: float32 [128, 512, 512], P('seq', 'hid')
- second_grad: float32 [512, 128, 128], P('seq', 'hid')
All inputs are finite; a program needn't handle non-finite values.
Results may differ from a plain program's by a relative error of at most 0.0061.
Values may be sent and summed in bfloat16 or wider, within the bound.
No kernel may reach another device: no remote copies, remote signals or barrier semaphores. Data moves between devices by JAX's collectives and lax.ppermute only.
A program may use at most 128 MiB of HBM per device.

v0:
```python
import jax
import jax.numpy as jnp
from jax import lax
from jax.sharding import Mesh
from jax.sharding import PartitionSpec as P

CHUNKS = 1
SEQ = ("zl", "x")
HID = ("zh", "y", "c")
PLANE = ("y", "c")
F32 = jnp.float32
BF16 = jnp.bfloat16


def swap(value, axes):
    return lax.all_to_all(value, axes, split_axis=0, concat_axis=0, tiled=True)


def gelu_slope(value):
    normal_cdf = 0.5 * (1.0 + jax.scipy.special.erf(value * 0.7071067811865476))
    density = jnp.exp(-0.5 * value * value) * 0.3989422804014327
    return normal_cdf + value * density


def dot(spec, left, right):
    return jnp.einsum(spec, left, right, preferred_element_type=F32)


def spread_second(blocks):
    group, panels = (blocks.shape[0], blocks.shape[1])
    width = group * panels
    rows = blocks.transpose(2, 0, 1).reshape(width, panels)
    col = lax.broadcasted_iota(jnp.int32, (panels, width), 1)
    pick = (col // group == lax.broadcasted_iota(jnp.int32, (panels, width), 0)).astype(BF16)
    full = dot("rb,bn->rn", rows, pick)
    at = lax.broadcasted_iota(jnp.int32, (width, width), 0) % group
    to = lax.broadcasted_iota(jnp.int32, (width, width), 1) % group
    return jnp.where(at == to, full, 0.0).astype(BF16)


def on_device(
    tokens,
    cotangent,
    seq_first,
    seq_second,
    feat_first,
    feature_second_blocks,
    gate_scale,
    gate_bias,
):
    n_seq, n_hid = (lax.axis_size(SEQ), lax.axis_size(HID))
    n_plane = lax.axis_size(PLANE)
    zh = lax.axis_index("zh")
    rows, width = tokens.shape
    blocks, block = (seq_first.shape[0], seq_first.shape[1])
    offs, nb = (seq_second.shape[0], seq_second.shape[1])
    groups, group = (feat_first.shape[0], feat_first.shape[1])
    per = offs // CHUNKS
    x_blocks = tokens.reshape(blocks, block, width)
    order = (n_seq, CHUNKS, per, blocks, width)
    x_rows = x_blocks.transpose(1, 0, 2).reshape(order)
    cot_rows = cotangent.reshape(blocks, block, width).transpose(1, 0, 2).reshape(order)
    second = seq_second.reshape(CHUNKS, per, nb, nb)
    eye = jnp.eye(groups, dtype=BF16)
    panel = (feat_first[:, :, None, :] * eye[:, None, :, None]).reshape(width, width)
    first = dot("qkj,qjc->kqc", seq_first, x_blocks).astype(BF16).reshape(order)
    x_plane = swap(x_blocks, PLANE).reshape(n_plane, block, width)
    spread = spread_second(lax.all_gather(feature_second_blocks, HID, axis=0, tiled=True))
    spread = spread.reshape(n_hid, width, n_hid, width)
    results, locals_, firsts, second_grads, first_grads = ([], [], [], [], [])
    for ch in range(CHUNKS):
        strided = swap(first[:, ch], SEQ).transpose(1, 0, 2, 3).reshape(per, nb, width)
        mixed_j = dot("jab,jbc->jac", second[ch], strided).astype(BF16)
        mixed_j = mixed_j.reshape(per, n_seq, blocks, width).transpose(1, 0, 2, 3)
        mixed = swap(mixed_j, SEQ).astype(F32)
        x_wide = x_rows[:, ch].astype(F32)
        cot = cot_rows[:, ch]
        gate = jax.nn.sigmoid(x_wide * gate_scale + gate_bias)
        hidden = (x_wide + gate * mixed).astype(BF16)
        inner = dot("sjqo,io->sjqi", hidden, panel).astype(BF16)
        by_row = (n_hid, per * blocks * n_seq // n_hid, width)
        cot_moved = swap(cot.reshape(by_row), HID)
        inner_moved = swap(inner.reshape(by_row), HID)
        inner_wide = inner_moved.astype(F32)
        act = jax.nn.gelu(inner_wide, approximate=False).astype(BF16)
        outer = dot("htc,hcdn->dtn", act, spread).astype(BF16)
        d_act = dot("dtn,hcdn->htc", cot_moved, spread)
        d_inner = (d_act * gelu_slope(inner_wide)).astype(BF16)
        d_back = swap(d_inner, HID).reshape(hidden.shape)
        d_hidden = cot.astype(F32) + dot("sjqi,io->sjqo", d_back, panel)
        d_mixed = (d_hidden * gate).astype(BF16)
        locals_.append(d_hidden * (1.0 + gate_scale * gate * (1.0 - gate) * mixed))
        d_mixed_j = swap(d_mixed, SEQ).transpose(1, 0, 2, 3).reshape(per, nb, width)
        d_first_j = dot("jab,jac->jbc", second[ch], d_mixed_j).astype(BF16)
        d_first_j = d_first_j.reshape(per, n_seq, blocks, width).transpose(1, 0, 2, 3)
        firsts.append(swap(d_first_j, SEQ))
        outer = swap(outer, HID).reshape(hidden.shape)
        results.append((hidden.astype(F32) + outer.astype(F32)).astype(BF16))
        part = dot("jac,jbc->jab", d_mixed_j, strided).astype(BF16)
        part = part.reshape(per, n_hid // n_plane, n_plane, nb // n_hid, nb)
        part = swap(part.transpose(2, 1, 0, 3, 4), PLANE)
        part = part.reshape(n_plane, n_hid // n_plane, per, nb // n_hid, nb).astype(F32).sum(0)
        keep = lax.dynamic_index_in_dim(part, zh, 0, keepdims=False)
        send = lax.dynamic_index_in_dim(part, 1 - zh, 0, keepdims=False)
        second_grads.append(keep + lax.ppermute(send, "zh", [(0, 1), (1, 0)]))
        d_first_q = firsts[ch].transpose(2, 0, 1, 3).reshape(blocks, n_seq * per, width)
        d_plane = swap(d_first_q, PLANE).reshape(n_plane, n_seq * per, width)
        prod = dot("skc,sjc->kj", d_plane, x_plane)
        prod = prod.reshape(n_hid // n_plane, n_plane, per, block)
        keep = lax.dynamic_index_in_dim(prod, zh, 0, keepdims=False)
        send = lax.dynamic_index_in_dim(prod, 1 - zh, 0, keepdims=False).astype(BF16)
        prod = keep + lax.ppermute(send, "zh", [(0, 1), (1, 0)]).astype(F32)
        first_grads.append(swap(prod, PLANE))

    def whole(parts):
        stacked = jnp.stack(parts, axis=1)
        return stacked.reshape(block, blocks, width).transpose(1, 0, 2).reshape(rows, width)

    d_first = jnp.stack(firsts, axis=1).reshape(block, blocks, width)
    seq_part = dot("qkj,kqc->qjc", seq_first, d_first).reshape(rows, width)
    token_grad = (seq_part + whole(locals_)).astype(BF16)
    first_grad = jnp.concatenate(first_grads, axis=1)
    second_grad = jnp.concatenate(second_grads, axis=0)
    return (whole(results), token_grad, first_grad, second_grad)


def solution(mesh):
    fine = Mesh(mesh.devices.reshape(4, 4, 2, 4, 2), ("zl", "x", "zh", "y", "c"))
    return jax.shard_map(
        on_device,
        mesh=fine,
        in_specs=(
            P(SEQ, HID),
            P(SEQ, HID),
            P(SEQ, None, None),
            P(SEQ, None, None),
            P(HID, None, None),
            P(HID, None, None),
            P(HID),
            P(HID),
        ),
        out_specs=(P(SEQ, HID), P(SEQ, HID), P(SEQ, HID, None), P(SEQ, HID, None)),
        check_vma=False,
    )
```

profile of v0, /device:TPU:32, one launch (start us, length us, event | category | flops | bytes accessed | tf_op | source)
XLA Modules:
  0.0 420.0 jit_solution(11952652844444209195)
XLA Ops:
  0.6 0.0 copy-start
  0.6 4.1 fusion.55
  4.8 0.8 copy.51
  5.5 34.3 %all_to_all.60 = bf16[16,32,8,128]{3,2,1,0:T(8,128)(2,1)S(1)} all-to-all(bf16[16,32,8,128]{3,2,1,0:T(8,128)(2,1)S(1)} %bitcast.158), channel_id=1, replica_groups=mesh['zl'=4,'x'=4,'zh'=2,'y'=4,'c'=2] {'zl','x'}, dimensions={0} | all-to-all | bytes 2097152 | tf_op jit(solution)/shard_map/all_to_all | solution.py:16
  39.8 0.4 fusion.58
  40.3 1.2 copy.116
  41.5 5.1 %all-to-all-start.1 = ((bf16[16,32,8,128]{3,2,1,0:T(8,128)(2,1)}), bf16[16,32,8,128]{3,2,1,0:T(8,128)(2,1)}, u32[]{:S(2)}, u32[]{:S(2)}) async-start(bf16[16,32,8,128]{3,2,1,0:T(8,128)(2,1)} %bitcast.143), calls=%async_computation.1 | async-start | bytes 2097152 | tf_op jit(solution)/shard_map/all_to_all | solution.py:16
  46.6 3.0 copy.60
  49.7 22.0 %all-to-all-done.1 = bf16[16,32,8,128]{3,2,1,0:T(8,128)(2,1)} async-done(((bf16[16,32,8,128]{3,2,1,0:T(8,128)(2,1)}), bf16[16,32,8,128]{3,2,1,0:T(8,128)(2,1)}, u32[]{:S(2)}, u32[]{:S(2)}) %all-to-all-start.1) | async-done | bytes 1048608 | tf_op jit(solution)/shard_map/all_to_all | solution.py:16
  71.7 8.6 %all-to-all-start.4 = ((bf16[16,256,128]{2,1,0:T(8,128)(2,1)}), bf16[16,256,128]{2,1,0:T(8,128)(2,1)}, u32[]{:S(2)}, u32[]{:S(2)}) async-start(bf16[16,256,128]{2,1,0:T(8,128)(2,1)} %bitcast.154), calls=%async_computation.4 | async-start | bytes 2097152 | tf_op jit(solution)/shard_map/all_to_all | solution.py:16
  80.2 0.1 convert_bitcast_fusion
  80.4 0.0 copy-start.9
  80.4 2.6 copy.49
  83.0 0.1 broadcast_multiply_fusion
  83.1 0.1 reshape.106
  83.2 2.5 fusion.7
  85.8 1.0 copy-done.3
  86.8 0.4 fusion.56
  87.2 1.3 copy.55
  88.5 23.0 %all-to-all-done.4 = bf16[16,256,128]{2,1,0:T(8,128)(2,1)} async-done(((bf16[16,256,128]{2,1,0:T(8,128)(2,1)}), bf16[16,256,128]{2,1,0:T(8,128)(2,1)}, u32[]{:S(2)}, u32[]{:S(2)}) %all-to-all-start.4) | async-done | bytes 1048608 | tf_op jit(solution)/shard_map/all_to_all | solution.py:16
  111.6 4.3 %all-to-all-start.2 = ((bf16[16,256,128]{1,2,0:T(8,128)(2,1)}), bf16[16,256,128]{1,2,0:T(8,128)(2,1)}, u32[]{:S(2)}, u32[]{:S(2)}) async-start(bf16[16,256,128]{1,2,0:T(8,128)(2,1)} %copy.55), calls=%async_computation.2 | async-start | bytes 2097152 | tf_op jit(solution)/shard_map/all_to_all | solution.py:16
  115.9 40.7 %all_gather.3 = bf16[64,32,32]{2,1,0:T(8,128)(2,1)S(1)} all-gather(bf16[4,32,32]{2,1,0:T(8,128)(2,1)S(1)} %copy-done.10), channel_id=1, replica_groups=mesh['zl'=4,'x'=4,'zh'=2,'y'=4,'c'=2] {'zh','y','c'}, dimensions={0}, use_global_device_ids=true | all-gather | bytes 139264 | tf_op jit(solution)/shard_map/all_gather | solution.py:68
  156.6 0.6 copy.54
  157.2 0.3 reshape.92
  157.5 5.2 %fusion.5 = bf16[256,8,16,128]{3,1,2,0:T(8,128)(2,1)} fusion(bf16[2048,32]{0,1:T(8,128)(2,1)S(1)} %reshape.92, s32[2048]{0:T(1024)S(1)} %get-tuple-element.7, s32[2048]{0:T(1024)S(1)} %get-tuple-element.8, pred[2048]{0:T(1024)(128)(4,1)S(1)} %get-tuple-element.11, s32[2048]{0:T(1024)S(1)} %get-tuple-element.6, s32[2048]{0:T(1024)S(1)} %get-tuple-element.9, ...), kind=kOutput, calls=%fused_computation.7 | convolution fusion | flops 289538048 | bytes 8556544 | tf_op jit(solution)/shard_map/rb,bn->rn/dot_general | solution.py:26
  162.7 9.8 %copy.82 = bf16[256,8,16,128]{3,2,1,0:T(8,128)(2,1)} copy(bf16[256,8,16,128]{3,1,2,0:T(8,128)(2,1)} %fusion.5) | data formatting | bytes 16777216
  172.5 8.1 %fusion.50 = bf16[16,256,128]{1,2,0:T(8,128)(2,1)S(1)} fusion(bf16[16,256,128]{1,2,0:T(8,128)(2,1)} %all-to-all-done.2, bf16[16,128,16,128]{1,0,3,2:T(8,128)(2,1)} %bitcast.151, bf16[16,256,128]{2,1,0:T(8,128)(2,1)} %all-to-all-done.4), kind=kOutput, calls=%fused_computation.69 | convolution fusion | flops 2153250816 | bytes 11534336 | tf_op jit(solution)/shard_map/dtn,hcdn->htc/dot_general | solution.py:26
  180.7 33.2 %all_to_all.61 = bf16[16,256,128]{1,2,0:T(8,128)(2,1)} all-to-all(bf16[16,256,128]{1,2,0:T(8,128)(2,1)S(1)} %fusion.50), channel_id=1, replica_groups=mesh['zl'=4,'x'=4,'zh'=2,'y'=4,'c'=2] {'zh','y','c'}, dimensions={0} | all-to-all | bytes 2097152 | tf_op jit(solution)/shard_map/all_to_all | solution.py:16
  213.9 2.3 copy.62
  216.2 4.8 %multiply_convert_fusion = (bf16[16,32,8,128]{3,2,1,0:T(8,128)(2,1)S(1)}, f32[16,32,8,128]{3,2,1,0:T(8,128)}) fusion(f32[128]{0:T(128)S(1)} %copy-done.11, f32[16,32,8,128]{3,2,1,0:T(8,128)} %bitcast.150, f32[128]{0:T(128)S(1)} %copy-done.12, bf16[16,32,8,128]{3,2,1,0:T(8,128)(2,1)} %all-to-all-done.1, bf16[128,128,1,1]{1,0,2,3:T(8,128)(2,1)S(1)} %reshape.106, ...), kind=kOutput, calls=%fused_computation.67 | convolution fusion | flops 142606336 | bytes 8422400 | tf_op jit(solution)/shard_map/sjqi,io->sjqo/dot_general | solution.py:26
  221.0 40.3 %all_to_all.62 = bf16[16,32,8,128]{3,2,1,0:T(8,128)(2,1)S(1)} all-to-all(bf16[16,32,8,128]{3,2,1,0:T(8,128)(2,1)S(1)} %get-tuple-element.4), channel_id=1, replica_groups=mesh['zl'=4,'x'=4,'zh'=2,'y'=4,'c'=2] {'zl','x'}, dimensions={0} | all-to-all | bytes 2097152 | tf_op jit(solution)/shard_map/all_to_all | solution.py:16
  261.3 4.3 %all-to-all-start.9 = ((bf16[8,512,128]{2,1,0:T(8,128)(2,1)}), bf16[8,512,128]{2,1,0:T(8,128)(2,1)}, u32[]{:S(2)}, u32[]{:S(2)}) async-start(bf16[8,512,128]{2,1,0:T(8,128)(2,1)} %bitcast.145), calls=%async_computation.9 | async-start | bytes 2097152 | tf_op jit(solution)/shard_map/all_to_all | solution.py:16
  265.6 0.5 fusion.57
  266.1 1.3 copy.115
  267.4 14.1 %all-to-all-done.9 = bf16[8,512,128]{2,1,0:T(8,128)(2,1)} async-done(((bf16[8,512,128]{2,1,0:T(8,128)(2,1)}), bf16[8,512,128]{2,1,0:T(8,128)(2,1)}, u32[]{:S(2)}, u32[]{:S(2)}) %all-to-all-start.9) | async-done | bytes 1048608 | tf_op jit(solution)/shard_map/all_to_all | solution.py:16
  281.5 5.1 %all-to-all-start.7 = ((bf16[16,32,8,128]{3,2,1,0:T(8,128)(2,1)}), bf16[16,32,8,128]{3,2,1,0:T(8,128)(2,1)S(1)}, u32[]{:S(2)}, u32[]{:S(2)}) async-start(bf16[16,32,8,128]{3,2,1,0:T(8,128)(2,1)} %bitcast.157), calls=%async_computation.7 | async-start | bytes 2097152 | tf_op jit(solution)/shard_map/all_to_all | solution.py:16
  286.6 11.6 %fusion.59 = bf16[16,256,128]{1,2,0:T(8,128)(2,1)} fusion(bf16[16,128,16,128]{1,0,3,2:T(8,128)(2,1)} %bitcast.152, bf16[16,256,128]{1,2,0:T(8,128)(2,1)} %all-to-all-done.2), kind=kOutput, calls=%fused_computation.79 | convolution fusion | flops 2182610944 | bytes 10485760 | tf_op jit(solution)/shard_map/htc,hcdn->dtn/dot_general | solution.py:26
  298.2 13.8 %all-to-all-done.7 = bf16[16,32,8,128]{3,2,1,0:T(8,128)(2,1)S(1)} async-done(((bf16[16,32,8,128]{3,2,1,0:T(8,128)(2,1)}), bf16[16,32,8,128]{3,2,1,0:T(8,128)(2,1)S(1)}, u32[]{:S(2)}, u32[]{:S(2)}) %all-to-all-start.7) | async-done | bytes 1048608 | tf_op jit(solution)/shard_map/all_to_all | solution.py:16
  312.0 4.3 %all-to-all-start.3 = ((bf16[16,256,128]{1,2,0:T(8,128)(2,1)}), bf16[16,256,128]{1,2,0:T(8,128)(2,1)}, u32[]{:S(2)}, u32[]{:S(2)}) async-start(bf16[16,256,128]{1,2,0:T(8,128)(2,1)} %fusion.59), calls=%async_computation.3 | async-start | bytes 2097152 | tf_op jit(solution)/shard_map/all_to_all | solution.py:16
  316.4 1.2 copy.69
  317.6 30.1 %all-to-all-done.3 = bf16[16,256,128]{1,2,0:T(8,128)(2,1)} async-done(((bf16[16,256,128]{1,2,0:T(8,128)(2,1)}), bf16[16,256,128]{1,2,0:T(8,128)(2,1)}, u32[]{:S(2)}, u32[]{:S(2)}) %all-to-all-start.3) | async-done | bytes 1048608 | tf_op jit(solution)/shard_map/all_to_all | solution.py:16
  347.6 4.2 %all-to-all-start.8 = ((bf16[8,512,128]{2,1,0:T(8,128)(2,1)}), bf16[8,512,128]{2,1,0:T(8,128)(2,1)}, u32[]{:S(2)}, u32[]{:S(2)}) async-start(bf16[8,512,128]{2,1,0:T(8,128)(2,1)} %bitcast.156), calls=%async_computation.8 | async-start | bytes 2097152 | tf_op jit(solution)/shard_map/all_to_all | solution.py:16
  351.9 0.8 convolution_convert_fusion.1
  352.7 1.2 copy.114
  354.0 13.9 %all-to-all-done.8 = bf16[8,512,128]{2,1,0:T(8,128)(2,1)} async-done(((bf16[8,512,128]{2,1,0:T(8,128)(2,1)}), bf16[8,512,128]{2,1,0:T(8,128)(2,1)}, u32[]{:S(2)}, u32[]{:S(2)}) %all-to-all-start.8) | async-done | bytes 1048608 | tf_op jit(solution)/shard_map/all_to_all | solution.py:16
  367.8 3.6 all-to-all-start.11
  371.4 2.7 copy.58
  374.1 1.9 fusion.49
  376.0 1.1 copy.59
  377.1 3.0 copy.67
  380.1 2.3 fusion.147
  382.4 0.8 fusion.105
  383.2 0.6 collective-permute-start
  383.7 3.5 all-to-all-done.11
  387.2 0.1 convert_reduce_fusion
  387.4 2.0 collective-permute-start.1
  389.4 11.9 %collective-permute-done = bf16[8,32,512]{2,1,0:T(8,128)(2,1)S(1)} collective-permute-done((bf16[8,32,512]{2,1,0:T(8,128)(2,1)}, bf16[8,32,512]{2,1,0:T(8,128)(2,1)S(1)}, u32[]{:S(2)}, u32[]{:S(2)}) %collective-permute-start) | collective-permute-done | bytes 262176 | tf_op jit(solution)/shard_map/ppermute | solution.py:112
  401.3 1.9 bitcast_add_fusion.2
  403.2 4.5 %all-to-all-start.10 = ((f32[8,32,512]{2,1,0:T(8,128)}), f32[8,32,512]{2,1,0:T(8,128)}, u32[]{:S(2)}, u32[]{:S(2)}) async-start(f32[8,32,512]{2,1,0:T(8,128)} %bitcast_add_fusion.2), calls=%async_computation.10 | async-start | bytes 1048576 | tf_op jit(solution)/shard_map/all_to_all | solution.py:16
  407.7 0.7 bitcast_add_fusion.3
  408.4 3.7 fusion.48
  412.1 1.3 copy.68
  413.4 4.7 %all-to-all-done.10 = f32[8,32,512]{2,1,0:T(8,128)} async-done(((f32[8,32,512]{2,1,0:T(8,128)}), f32[8,32,512]{2,1,0:T(8,128)}, u32[]{:S(2)}, u32[]{:S(2)}) %all-to-all-start.10) | async-done | bytes 524320 | tf_op jit(solution)/shard_map/all_to_all | solution.py:16
  418.1 1.9 copy.118
  (30 shorter events, 0.1 us)
Async XLA Ops:
  0.6 39.2 %copy-start = (bf16[32,128,128]{2,1,0:T(8,128)(2,1)S(1)}, bf16[32,128,128]{2,1,0:T(8,128)(2,1)}, u32[]{:S(2)}) copy-start(bf16[32,128,128]{2,1,0:T(8,128)(2,1)} %param.11) | copy-start | bytes 3145732
  41.5 30.2 %all-to-all-start.1 = ((bf16[16,32,8,128]{3,2,1,0:T(8,128)(2,1)}), bf16[16,32,8,128]{3,2,1,0:T(8,128)(2,1)}, u32[]{:S(2)}, u32[]{:S(2)}) async-start(bf16[16,32,8,128]{3,2,1,0:T(8,128)(2,1)} %bitcast.143), calls=%async_computation.1 | async-start | bytes 2097152 | tf_op jit(solution)/shard_map/all_to_all | solution.py:16
  46.6 33.6 %copy-start.2 = (bf16[4096,128]{1,0:T(8,128)(2,1)S(1)}, bf16[4096,128]{1,0:T(8,128)(2,1)}, u32[]{:S(2)}) copy-start(bf16[4096,128]{1,0:T(8,128)(2,1)} %param.8) | copy-start | bytes 3145732
  71.7 39.9 %all-to-all-start.4 = ((bf16[16,256,128]{2,1,0:T(8,128)(2,1)}), bf16[16,256,128]{2,1,0:T(8,128)(2,1)}, u32[]{:S(2)}, u32[]{:S(2)}) async-start(bf16[16,256,128]{2,1,0:T(8,128)(2,1)} %bitcast.154), calls=%async_computation.4 | async-start | bytes 2097152 | tf_op jit(solution)/shard_map/all_to_all | solution.py:16
  80.4 2.6 copy-start.9
  80.4 2.8 copy-start.11
  80.4 2.8 copy-start.12
  85.8 1.0 copy-start.3
  87.2 28.7 %copy-start.10 = (bf16[4,32,32]{2,1,0:T(8,128)(2,1)S(1)}, bf16[4,32,32]{2,1,0:T(8,128)(2,1)}, u32[]{:S(2)}) copy-start(bf16[4,32,32]{2,1,0:T(8,128)(2,1)} %param.13) | copy-start | bytes 24580
  111.6 61.0 %all-to-all-start.2 = ((bf16[16,256,128]{1,2,0:T(8,128)(2,1)}), bf16[16,256,128]{1,2,0:T(8,128)(2,1)}, u32[]{:S(2)}, u32[]{:S(2)}) async-start(bf16[16,256,128]{1,2,0:T(8,128)(2,1)} %copy.55), calls=%async_computation.2 | async-start | bytes 2097152 | tf_op jit(solution)/shard_map/all_to_all | solution.py:16
  180.7 35.5 %copy-start.7 = (bf16[8,512,128]{2,0,1:T(8,128)(2,1)S(1)}, bf16[8,512,128]{2,0,1:T(8,128)(2,1)}, u32[]{:S(2)}) copy-start(bf16[8,512,128]{2,0,1:T(8,128)(2,1)} %copy.60) | copy-start | bytes 3145732
  261.3 20.2 %all-to-all-start.9 = ((bf16[8,512,128]{2,1,0:T(8,128)(2,1)}), bf16[8,512,128]{2,1,0:T(8,128)(2,1)}, u32[]{:S(2)}, u32[]{:S(2)}) async-start(bf16[8,512,128]{2,1,0:T(8,128)(2,1)} %bitcast.145), calls=%async_computation.9 | async-start | bytes 2097152 | tf_op jit(solution)/shard_map/all_to_all | solution.py:16
  281.5 30.5 %all-to-all-start.7 = ((bf16[16,32,8,128]{3,2,1,0:T(8,128)(2,1)}), bf16[16,32,8,128]{3,2,1,0:T(8,128)(2,1)S(1)}, u32[]{:S(2)}, u32[]{:S(2)}) async-start(bf16[16,32,8,128]{3,2,1,0:T(8,128)(2,1)} %bitcast.157), calls=%async_computation.7 | async-start | bytes 2097152 | tf_op jit(solution)/shard_map/all_to_all | solution.py:16
  312.0 5.5 %copy-start.5 = (bf16[16,32,8,128]{3,2,1,0:T(8,128)(2,1)}, bf16[16,32,8,128]{3,2,1,0:T(8,128)(2,1)S(1)}, u32[]{:S(2)}) copy-start(bf16[16,32,8,128]{3,2,1,0:T(8,128)(2,1)S(1)} %all-to-all-done.7) | copy-start | bytes 3145732
  312.0 35.6 %all-to-all-start.3 = ((bf16[16,256,128]{1,2,0:T(8,128)(2,1)}), bf16[16,256,128]{1,2,0:T(8,128)(2,1)}, u32[]{:S(2)}, u32[]{:S(2)}) async-start(bf16[16,256,128]{1,2,0:T(8,128)(2,1)} %fusion.59), calls=%async_computation.3 | async-start | bytes 2097152 | tf_op jit(solution)/shard_map/all_to_all | solution.py:16
  347.6 20.2 %all-to-all-start.8 = ((bf16[8,512,128]{2,1,0:T(8,128)(2,1)}), bf16[8,512,128]{2,1,0:T(8,128)(2,1)}, u32[]{:S(2)}, u32[]{:S(2)}) async-start(bf16[8,512,128]{2,1,0:T(8,128)(2,1)} %bitcast.156), calls=%async_computation.8 | async-start | bytes 2097152 | tf_op jit(solution)/shard_map/all_to_all | solution.py:16
  367.8 19.4 %all-to-all-start.11 = ((bf16[8,2,32,8,128]{4,3,1,2,0:T(8,128)(2,1)}), bf16[8,2,32,8,128]{4,3,1,2,0:T(8,128)(2,1)S(1)}, u32[]{:S(2)}, u32[]{:S(2)}) async-start(bf16[8,2,32,8,128]{4,3,1,2,0:T(8,128)(2,1)} %bitcast.141), calls=%async_computation.11 | async-start | bytes 2097152 | tf_op jit(solution)/shard_map/all_to_all | solution.py:16
  371.4 2.7 copy-start.4
  382.4 1.4 copy-start.8
  383.2 25.2 %copy-start.6 = (bf16[16,32,8,128]{3,2,1,0:T(8,128)(2,1)S(1)}, bf16[16,32,8,128]{3,2,1,0:T(8,128)(2,1)}, u32[]{:S(2)}) copy-start(bf16[16,32,8,128]{3,2,1,0:T(8,128)(2,1)} %copy-done.5) | copy-start | bytes 3145732
  383.2 18.1 %collective-permute-start = (bf16[8,32,512]{2,1,0:T(8,128)(2,1)}, bf16[8,32,512]{2,1,0:T(8,128)(2,1)S(1)}, u32[]{:S(2)}, u32[]{:S(2)}) collective-permute-start(bf16[8,32,512]{2,1,0:T(8,128)(2,1)} %fusion.105), channel_id=1, source_target_pairs={{0,8},{8,0},{1,9},{9,1},{2,10},{10,2},{3,11},{11,3},{4,12},{12,4},... | collective-permute-start | bytes 786440 | tf_op jit(solution)/shard_map/ppermute | solution.py:112
  387.4 20.3 %collective-permute-start.1 = (f32[32,8,128]{2,1,0:T(8,128)S(1)}, f32[32,8,128]{2,1,0:T(8,128)S(1)}, u32[]{:S(2)}, u32[]{:S(2)}) collective-permute-start(f32[32,8,128]{2,1,0:T(8,128)S(1)} %dynamic-slice_bitcast_fusion), channel_id=1, source_target_pairs={{0,8},{8,0},{1,9},{9,1},{2,10},{10,2},{3,11},{11,3},{4,12},{12,4},... | collective-permute-start | bytes 393224 | tf_op jit(solution)/shard_map/ppermute | solution.py:105
  403.2 14.9 %all-to-all-start.10 = ((f32[8,32,512]{2,1,0:T(8,128)}), f32[8,32,512]{2,1,0:T(8,128)}, u32[]{:S(2)}, u32[]{:S(2)}) async-start(f32[8,32,512]{2,1,0:T(8,128)} %bitcast_add_fusion.2), calls=%async_computation.10 | async-start | bytes 1048576 | tf_op jit(solution)/shard_map/all_to_all | solution.py:16
  408.4 11.6 %copy-start.1 = (bf16[32,128,128]{2,1,0:T(8,128)(2,1)S(1)}, bf16[32,128,128]{2,1,0:T(8,128)(2,1)}, u32[]{:S(2)}) copy-start(bf16[32,128,128]{2,1,0:T(8,128)(2,1)} %param.11) | copy-start | bytes 3145732
where the time goes:
time: 421 us; the launch traced here: 420 us
  blocking collectives  148 us (35%)
  waiting for transfers between devices  137 us (33%)
  starting transfers between devices  46.5 us (11%)
  matrix products  42.2 us (10%)
  local copies, waits for them, and re-layouts  37.5 us (9%)
  other arithmetic  7.41 us (2%)
    all_to_all x9, waiting for transfers between devices, swap(): return lax.all_to_all(value, axes, split_axis=0, concat_axis=0, tiled=True)  125 us
    all_to_all x3, blocking collectives, swap(): return lax.all_to_all(value, axes, split_axis=0, concat_axis=0, tiled=True)  108 us
    all_to_all x9, starting transfers between devices, swap(): return lax.all_to_all(value, axes, split_axis=0, concat_axis=0, tiled=True)  44 us
    dot_general x11, matrix products, dot(): return jnp.einsum(spec, left, right, preferred_element_type=F32)  42.2 us
    all_gather x1, blocking collectives, on_device(): lax.all_gather(feature_second_blocks, HID, axis=0, tiled=True)  40.7 us
    unnamed x28, local copies, waits for them, and re-layouts  12.7 us
    ppermute x1, waiting for transfers between devices, on_device(): prod = keep + lax.ppermute(send, 'zh', [(0, 1), (1, 0)]).astype(F32)  11.9 us
  transfers between devices with their start and end apart: 11, of which 9 were waited for; matrix products, arithmetic and copies ran while one was open for 15% of the time, Pallas kernels for 0%

commit v1 on v0

--- a/solution.py
+++ b/solution.py
@@ -3,6 +3,7 @@
 from jax import lax
 from jax.sharding import Mesh
 from jax.sharding import PartitionSpec as P
+from jax.lax import all_to_all, psum
 
 CHUNKS = 1
 SEQ = ("zl", "x")
@@ -10,6 +11,16 @@
 PLANE = ("y", "c")
 F32 = jnp.float32
 BF16 = jnp.bfloat16
+
+
+def apply_map_up(xin):
+    w_next = jnp.concatenate(
+        all_to_all(
+            jnp.stack(psum(1, axis_name=HID) * [xin], 0), axis_name=HID, split_axis=0, concat_axis=0
+        ),
+        0,
+    )
+    return w_next
 
 
 def swap(value, axes):
@@ -65,7 +76,7 @@
     panel = (feat_first[:, :, None, :] * eye[:, None, :, None]).reshape(width, width)
     first = dot("qkj,qjc->kqc", seq_first, x_blocks).astype(BF16).reshape(order)
     x_plane = swap(x_blocks, PLANE).reshape(n_plane, block, width)
-    spread = spread_second(lax.all_gather(feature_second_blocks, HID, axis=0, tiled=True))
+    spread = spread_second(apply_map_up(feature_second_blocks))
     spread = spread.reshape(n_hid, width, n_hid, width)
     results, locals_, firsts, second_grads, first_grads = ([], [], [], [], [])
     for ch in range(CHUNKS):

time: 421 us -> 401 us (0.952)
  blocking collectives: 148 us -> 65.1 us
  waiting for transfers between devices: 137 us -> 184 us
  starting transfers between devices: 46.5 us -> 59.8 us
    all_to_all x3 -> x2, blocking collectives: 108 us -> 65.1 us  [swap(): return lax.all_to_all(value, axes, split_axis=0, concat_axis=0, tiled=True)]
    all_gather x1 -> x0, blocking collectives: 40.7 us -> none  [on_device(): lax.all_gather(feature_second_blocks, HID, axis=0, tiled=True)]
    all_to_all x9 -> x10, waiting for transfers between devices: 125 us -> 163 us  [swap(): return lax.all_to_all(value, axes, split_axis=0, concat_axis=0, tiled=True)]
    all_to_all x0 -> x1, waiting for transfers between devices: none -> 9.87 us  [apply_map_up(): all_to_all(jnp.stack(psum(1, axis_name=HID) * [xin], 0), axis_name=HID, s...]
    all_to_all x0 -> x1, starting transfers between devices: none -> 8.5 us  [apply_map_up(): all_to_all(jnp.stack(psum(1, axis_name=HID) * [xin], 0), axis_name=HID, s...]
    all_to_all x9 -> x10, starting transfers between devices: 44 us -> 48.7 us  [swap(): return lax.all_to_all(value, axes, split_axis=0, concat_axis=0, tiled=True)]
    unnamed x28 -> x30, local copies, waits for them, and re-layouts: 12.7 us -> 14.2 us
  transfers between devices with their start and end apart: 11 -> 13, of which waited for: 9 -> 12; matrix products, arithmetic and copies ran while one was open for 15% -> 16% of each run, Pallas kernels for 0% -> 0%
where the time goes in v1:
time: 401 us; the launch traced here: 399 us
  waiting for transfers between devices  184 us (46%)
  blocking collectives  65.1 us (16%)
  starting transfers between devices  59.8 us (15%)
  matrix products  42.2 us (11%)
  local copies, waits for them, and re-layouts  39.7 us (10%)
  other arithmetic  7.41 us (2%)
    all_to_all x10, waiting for transfers between devices, swap(): return lax.all_to_all(value, axes, split_axis=0, concat_axis=0, tiled=True)  163 us
    all_to_all x2, blocking collectives, swap(): return lax.all_to_all(value, axes, split_axis=0, concat_axis=0, tiled=True)  65.1 us
    all_to_all x10, starting transfers between devices, swap(): return lax.all_to_all(value, axes, split_axis=0, concat_axis=0, tiled=True)  48.7 us
    dot_general x11, matrix products, dot(): return jnp.einsum(spec, left, right, preferred_element_type=F32)  42.2 us
    unnamed x30, local copies, waits for them, and re-layouts  14.2 us
    ppermute x1, waiting for transfers between devices, on_device(): prod = keep + lax.ppermute(send, 'zh', [(0, 1), (1, 0)]).astype(F32)  11.9 us
    all_to_all x1, waiting for transfers between devices, apply_map_up(): all_to_all(jnp.stack(psum(1, axis_name=HID) * [xin], 0), axis_name=HID, s...  9.87 us
    all_to_all x1, starting transfers between devices, apply_map_up(): all_to_all(jnp.stack(psum(1, axis_name=HID) * [xin], 0), axis_name=HID, s...  8.5 us
  transfers between devices with their start and end apart: 13, of which 12 were waited for; matrix products, arithmetic and copies ran while one was open for 16% of the time, Pallas kernels for 0%

profile of v1, /device:TPU:32, one launch (start us, length us, event | category | flops | bytes accessed | tf_op | source)
XLA Modules:
  0.0 399.5 jit_solution(6285050712112846602)
XLA Ops:
  0.6 4.1 %fusion.55 = bf16[512,8,128]{0,2,1:T(8,128)(2,1)S(1)} fusion(bf16[8,512,128]{2,1,0:T(8,128)(2,1)} %bitcast.146, bf16[8,512,512]{2,1,0:T(8,128)(2,1)} %param.10), kind=kOutput, calls=%fused_computation.75 | convolution fusion | flops 537395200 | bytes 6291456 | tf_op jit(solution)/shard_map/qkj,qjc->kqc/dot_general | solution.py:37
  4.8 1.5 copy.72
  6.2 8.5 %all-to-all-start = ((bf16[16,32,8,128]{3,2,1,0:T(8,128)(2,1)}), bf16[16,32,8,128]{3,2,1,0:T(8,128)(2,1)S(1)}, u32[]{:S(2)}, u32[]{:S(2)}) async-start(bf16[16,32,8,128]{3,2,1,0:T(8,128)(2,1)} %bitcast.4), calls=%async_computation | async-start | bytes 2097152 | tf_op jit(solution)/shard_map/all_to_all | solution.py:27
  14.8 1.2 reshape.119
  16.0 24.4 %all-to-all-done = bf16[16,32,8,128]{3,2,1,0:T(8,128)(2,1)S(1)} async-done(((bf16[16,32,8,128]{3,2,1,0:T(8,128)(2,1)}), bf16[16,32,8,128]{3,2,1,0:T(8,128)(2,1)S(1)}, u32[]{:S(2)}, u32[]{:S(2)}) %all-to-all-start) | async-done | bytes 1048608 | tf_op jit(solution)/shard_map/all_to_all | solution.py:27
  40.4 8.5 %all-to-all-start.2 = ((bf16[16,2,2048]{2,1,0:T(2,128)(2,1)}), bf16[16,2,2048]{2,1,0:T(2,128)(2,1)S(1)}, u32[]{:S(2)}, u32[]{:S(2)}) async-start(bf16[16,2,2048]{2,1,0:T(2,128)(2,1)} %reshape.119), calls=%async_computation.2 | async-start | bytes 262144 | tf_op jit(solution)/shard_map/all_to_all | solution.py:18
  49.0 0.4 fusion.58
  49.4 1.2 copy.137
  50.6 9.9 %all-to-all-done.2 = bf16[16,2,2048]{2,1,0:T(2,128)(2,1)S(1)} async-done(((bf16[16,2,2048]{2,1,0:T(2,128)(2,1)}), bf16[16,2,2048]{2,1,0:T(2,128)(2,1)S(1)}, u32[]{:S(2)}, u32[]{:S(2)}) %all-to-all-start.2) | async-done | bytes 131104 | tf_op jit(solution)/shard_map/all_to_all | solution.py:18
  60.5 5.3 %all-to-all-start.1 = ((bf16[16,32,8,128]{3,2,1,0:T(8,128)(2,1)}), bf16[16,32,8,128]{3,2,1,0:T(8,128)(2,1)}, u32[]{:S(2)}, u32[]{:S(2)}) async-start(bf16[16,32,8,128]{3,2,1,0:T(8,128)(2,1)} %bitcast.145), calls=%async_computation.1 | async-start | bytes 2097152 | tf_op jit(solution)/shard_map/all_to_all | solution.py:27
  65.9 3.0 copy.81
  68.9 22.8 %all-to-all-done.1 = bf16[16,32,8,128]{3,2,1,0:T(8,128)(2,1)} async-done(((bf16[16,32,8,128]{3,2,1,0:T(8,128)(2,1)}), bf16[16,32,8,128]{3,2,1,0:T(8,128)(2,1)}, u32[]{:S(2)}, u32[]{:S(2)}) %all-to-all-start.1) | async-done | bytes 1048608 | tf_op jit(solution)/shard_map/all_to_all | solution.py:27
  91.7 4.4 %all-to-all-start.5 = ((bf16[16,256,128]{2,1,0:T(8,128)(2,1)}), bf16[16,256,128]{2,1,0:T(8,128)(2,1)}, u32[]{:S(2)}, u32[]{:S(2)}) async-start(bf16[16,256,128]{2,1,0:T(8,128)(2,1)} %bitcast.156), calls=%async_computation.5 | async-start | bytes 2097152 | tf_op jit(solution)/shard_map/all_to_all | solution.py:27
  96.2 2.6 copy.70
  99.1 2.5 fusion.7
  101.6 1.0 copy-done.3
  102.6 0.4 fusion.56
  103.0 1.3 copy.76
  104.4 22.9 %all-to-all-done.5 = bf16[16,256,128]{2,1,0:T(8,128)(2,1)} async-done(((bf16[16,256,128]{2,1,0:T(8,128)(2,1)}), bf16[16,256,128]{2,1,0:T(8,128)(2,1)}, u32[]{:S(2)}, u32[]{:S(2)}) %all-to-all-start.5) | async-done | bytes 1048608 | tf_op jit(solution)/shard_map/all_to_all | solution.py:27
  127.3 4.5 %all-to-all-start.3 = ((bf16[16,256,128]{1,2,0:T(8,128)(2,1)}), bf16[16,256,128]{1,2,0:T(8,128)(2,1)}, u32[]{:S(2)}, u32[]{:S(2)}) async-start(bf16[16,256,128]{1,2,0:T(8,128)(2,1)} %copy.76), calls=%async_computation.3 | async-start | bytes 2097152 | tf_op jit(solution)/shard_map/all_to_all | solution.py:27
  131.9 0.3 reshape.120
  132.1 0.6 copy.75
  132.7 0.3 reshape.98
  133.0 5.2 %fusion.5 = bf16[256,8,16,128]{3,1,2,0:T(8,128)(2,1)} fusion(bf16[2048,32]{0,1:T(8,128)(2,1)S(1)} %reshape.98, s32[2048]{0:T(1024)S(1)} %get-tuple-element.7, s32[2048]{0:T(1024)S(1)} %get-tuple-element.8, pred[2048]{0:T(1024)(128)(4,1)S(1)} %get-tuple-element.11, s32[2048]{0:T(1024)S(1)} %get-tuple-element.6, s32[2048]{0:T(1024)S(1)} %get-tuple-element.9, ...), kind=kOutput, calls=%fused_computation.7 | convolution fusion | flops 289538048 | bytes 8556544 | tf_op jit(solution)/shard_map/rb,bn->rn/dot_general | solution.py:37
  138.2 9.8 %copy.103 = bf16[256,8,16,128]{3,2,1,0:T(8,128)(2,1)} copy(bf16[256,8,16,128]{3,1,2,0:T(8,128)(2,1)} %fusion.5) | data formatting | bytes 16777216
  148.0 12.3 %all-to-all-done.3 = bf16[16,256,128]{1,2,0:T(8,128)(2,1)} async-done(((bf16[16,256,128]{1,2,0:T(8,128)(2,1)}), bf16[16,256,128]{1,2,0:T(8,128)(2,1)}, u32[]{:S(2)}, u32[]{:S(2)}) %all-to-all-start.3) | async-done | bytes 1048608 | tf_op jit(solution)/shard_map/all_to_all | solution.py:27
  160.4 8.1 %fusion.50 = bf16[16,256,128]{1,2,0:T(8,128)(2,1)S(1)} fusion(bf16[16,256,128]{1,2,0:T(8,128)(2,1)} %all-to-all-done.3, bf16[16,128,16,128]{1,0,3,2:T(8,128)(2,1)} %bitcast.153, bf16[16,256,128]{2,1,0:T(8,128)(2,1)} %all-to-all-done.5), kind=kOutput, calls=%fused_computation.69 | convolution fusion | flops 2153250816 | bytes 11534336 | tf_op jit(solution)/shard_map/dtn,hcdn->htc/dot_general | solution.py:37
  168.5 33.0 %all_to_all.65 = bf16[16,256,128]{1,2,0:T(8,128)(2,1)} all-to-all(bf16[16,256,128]{1,2,0:T(8,128)(2,1)S(1)} %fusion.50), channel_id=1, replica_groups=mesh['zl'=4,'x'=4,'zh'=2,'y'=4,'c'=2] {'zh','y','c'}, dimensions={0} | all-to-all | bytes 2097152 | tf_op jit(solution)/shard_map/all_to_all | solution.py:27
  201.5 2.3 copy.83
  203.7 4.9 %multiply_convert_fusion = (bf16[16,32,8,128]{3,2,1,0:T(8,128)(2,1)S(1)}, f32[16,32,8,128]{3,2,1,0:T(8,128)}) fusion(f32[128]{0:T(128)S(1)} %copy-done.11, f32[16,32,8,128]{3,2,1,0:T(8,128)} %bitcast.152, f32[128]{0:T(128)S(1)} %copy-done.12, bf16[16,32,8,128]{3,2,1,0:T(8,128)(2,1)} %all-to-all-done.1, bf16[128,128,1,1]{1,0,2,3:T(8,128)(2,1)S(1)} %reshape.112, ...), kind=kOutput, calls=%fused_computation.67 | convolution fusion | flops 142606336 | bytes 8422400 | tf_op jit(solution)/shard_map/sjqi,io->sjqo/dot_general | solution.py:37
  208.6 32.2 %all_to_all.66 = bf16[16,32,8,128]{3,2,1,0:T(8,128)(2,1)S(1)} all-to-all(bf16[16,32,8,128]{3,2,1,0:T(8,128)(2,1)S(1)} %get-tuple-element.4), channel_id=1, replica_groups=mesh['zl'=4,'x'=4,'zh'=2,'y'=4,'c'=2] {'zl','x'}, dimensions={0} | all-to-all | bytes 2097152 | tf_op jit(solution)/shard_map/all_to_all | solution.py:27
  240.8 4.3 %all-to-all-start.10 = ((bf16[8,512,128]{2,1,0:T(8,128)(2,1)}), bf16[8,512,128]{2,1,0:T(8,128)(2,1)}, u32[]{:S(2)}, u32[]{:S(2)}) async-start(bf16[8,512,128]{2,1,0:T(8,128)(2,1)} %bitcast.147), calls=%async_computation.10 | async-start | bytes 2097152 | tf_op jit(solution)/shard_map/all_to_all | solution.py:27
  245.0 0.5 fusion.57
  245.6 1.3 copy.136
  246.9 14.1 %all-to-all-done.10 = bf16[8,512,128]{2,1,0:T(8,128)(2,1)} async-done(((bf16[8,512,128]{2,1,0:T(8,128)(2,1)}), bf16[8,512,128]{2,1,0:T(8,128)(2,1)}, u32[]{:S(2)}, u32[]{:S(2)}) %all-to-all-start.10) | async-done | bytes 1048608 | tf_op jit(solution)/shard_map/all_to_all | solution.py:27
  261.0 5.1 %all-to-all-start.8 = ((bf16[16,32,8,128]{3,2,1,0:T(8,128)(2,1)}), bf16[16,32,8,128]{3,2,1,0:T(8,128)(2,1)S(1)}, u32[]{:S(2)}, u32[]{:S(2)}) async-start(bf16[16,32,8,128]{3,2,1,0:T(8,128)(2,1)} %bitcast.159), calls=%async_computation.8 | async-start | bytes 2097152 | tf_op jit(solution)/shard_map/all_to_all | solution.py:27
  266.1 11.6 %fusion.59 = bf16[16,256,128]{1,2,0:T(8,128)(2,1)} fusion(bf16[16,128,16,128]{1,0,3,2:T(8,128)(2,1)} %bitcast.154, bf16[16,256,128]{1,2,0:T(8,128)(2,1)} %all-to-all-done.3), kind=kOutput, calls=%fused_computation.79 | convolution fusion | flops 2182610944 | bytes 10485760 | tf_op jit(solution)/shard_map/htc,hcdn->dtn/dot_general | solution.py:37
  277.7 13.8 %all-to-all-done.8 = bf16[16,32,8,128]{3,2,1,0:T(8,128)(2,1)S(1)} async-done(((bf16[16,32,8,128]{3,2,1,0:T(8,128)(2,1)}), bf16[16,32,8,128]{3,2,1,0:T(8,128)(2,1)S(1)}, u32[]{:S(2)}, u32[]{:S(2)}) %all-to-all-start.8) | async-done | bytes 1048608 | tf_op jit(solution)/shard_map/all_to_all | solution.py:27
  291.5 4.4 %all-to-all-start.4 = ((bf16[16,256,128]{1,2,0:T(8,128)(2,1)}), bf16[16,256,128]{1,2,0:T(8,128)(2,1)}, u32[]{:S(2)}, u32[]{:S(2)}) async-start(bf16[16,256,128]{1,2,0:T(8,128)(2,1)} %fusion.59), calls=%async_computation.4 | async-start | bytes 2097152 | tf_op jit(solution)/shard_map/all_to_all | solution.py:27
  295.9 1.2 copy.90
  297.0 30.1 %all-to-all-done.4 = bf16[16,256,128]{1,2,0:T(8,128)(2,1)} async-done(((bf16[16,256,128]{1,2,0:T(8,128)(2,1)}), bf16[16,256,128]{1,2,0:T(8,128)(2,1)}, u32[]{:S(2)}, u32[]{:S(2)}) %all-to-all-start.4) | async-done | bytes 1048608 | tf_op jit(solution)/shard_map/all_to_all | solution.py:27
  327.1 4.2 %all-to-all-start.9 = ((bf16[8,512,128]{2,1,0:T(8,128)(2,1)}), bf16[8,512,128]{2,1,0:T(8,128)(2,1)}, u32[]{:S(2)}, u32[]{:S(2)}) async-start(bf16[8,512,128]{2,1,0:T(8,128)(2,1)} %bitcast.158), calls=%async_computation.9 | async-start | bytes 2097152 | tf_op jit(solution)/shard_map/all_to_all | solution.py:27
  331.4 0.8 convolution_convert_fusion.1
  332.2 1.2 copy.135
  333.4 13.9 %all-to-all-done.9 = bf16[8,512,128]{2,1,0:T(8,128)(2,1)} async-done(((bf16[8,512,128]{2,1,0:T(8,128)(2,1)}), bf16[8,512,128]{2,1,0:T(8,128)(2,1)}, u32[]{:S(2)}, u32[]{:S(2)}) %all-to-all-start.9) | async-done | bytes 1048608 | tf_op jit(solution)/shard_map/all_to_all | solution.py:27
  347.3 3.6 all-to-all-start.12
  350.9 2.7 copy.79
  353.6 1.9 fusion.49
  355.5 1.1 copy.80
  356.6 3.0 copy.88
  359.6 2.3 fusion.147
  361.9 0.8 fusion.105
  362.7 0.6 collective-permute-start
  363.2 3.5 all-to-all-done.12
  366.7 0.1 convert_reduce_fusion
  366.9 2.0 collective-permute-start.1
  368.9 11.9 %collective-permute-done = bf16[8,32,512]{2,1,0:T(8,128)(2,1)S(1)} collective-permute-done((bf16[8,32,512]{2,1,0:T(8,128)(2,1)}, bf16[8,32,512]{2,1,0:T(8,128)(2,1)S(1)}, u32[]{:S(2)}, u32[]{:S(2)}) %collective-permute-start) | collective-permute-done | bytes 262176 | tf_op jit(solution)/shard_map/ppermute | solution.py:123
  380.8 1.9 bitcast_add_fusion.2
  382.7 4.5 %all-to-all-start.11 = ((f32[8,32,512]{2,1,0:T(8,128)}), f32[8,32,512]{2,1,0:T(8,128)}, u32[]{:S(2)}, u32[]{:S(2)}) async-start(f32[8,32,512]{2,1,0:T(8,128)} %bitcast_add_fusion.2), calls=%async_computation.11 | async-start | bytes 1048576 | tf_op jit(solution)/shard_map/all_to_all | solution.py:27
  387.2 0.7 bitcast_add_fusion.3
  387.9 3.7 fusion.48
  391.6 1.3 copy.89
  392.9 4.7 %all-to-all-done.11 = f32[8,32,512]{2,1,0:T(8,128)} async-done(((f32[8,32,512]{2,1,0:T(8,128)}), f32[8,32,512]{2,1,0:T(8,128)}, u32[]{:S(2)}, u32[]{:S(2)}) %all-to-all-start.11) | async-done | bytes 524320 | tf_op jit(solution)/shard_map/all_to_all | solution.py:27
  397.6 1.9 copy.139
  (35 shorter events, 0.6 us)
Async XLA Ops:
  0.6 48.3 %copy-start = (bf16[32,128,128]{2,1,0:T(8,128)(2,1)S(1)}, bf16[32,128,128]{2,1,0:T(8,128)(2,1)}, u32[]{:S(2)}) copy-start(bf16[32,128,128]{2,1,0:T(8,128)(2,1)} %param.11) | copy-start | bytes 3145732
  4.8 10.0 %copy-start.9 = (bf16[4,32,32]{2,1,0:T(8,128)(2,1)S(1)}, bf16[4,32,32]{2,1,0:T(8,128)(2,1)}, u32[]{:S(2)}) copy-start(bf16[4,32,32]{2,1,0:T(8,128)(2,1)} %param.13) | copy-start | bytes 24580
  6.2 34.2 %all-to-all-start = ((bf16[16,32,8,128]{3,2,1,0:T(8,128)(2,1)}), bf16[16,32,8,128]{3,2,1,0:T(8,128)(2,1)S(1)}, u32[]{:S(2)}, u32[]{:S(2)}) async-start(bf16[16,32,8,128]{3,2,1,0:T(8,128)(2,1)} %bitcast.4), calls=%async_computation | async-start | bytes 2097152 | tf_op jit(solution)/shard_map/all_to_all | solution.py:27
  40.4 20.1 %all-to-all-start.2 = ((bf16[16,2,2048]{2,1,0:T(2,128)(2,1)}), bf16[16,2,2048]{2,1,0:T(2,128)(2,1)S(1)}, u32[]{:S(2)}, u32[]{:S(2)}) async-start(bf16[16,2,2048]{2,1,0:T(2,128)(2,1)} %reshape.119), calls=%async_computation.2 | async-start | bytes 262144 | tf_op jit(solution)/shard_map/all_to_all | solution.py:18
  60.5 31.2 %all-to-all-start.1 = ((bf16[16,32,8,128]{3,2,1,0:T(8,128)(2,1)}), bf16[16,32,8,128]{3,2,1,0:T(8,128)(2,1)}, u32[]{:S(2)}, u32[]{:S(2)}) async-start(bf16[16,32,8,128]{3,2,1,0:T(8,128)(2,1)} %bitcast.145), calls=%async_computation.1 | async-start | bytes 2097152 | tf_op jit(solution)/shard_map/all_to_all | solution.py:27
  65.8 30.2 %copy-start.2 = (bf16[4096,128]{1,0:T(8,128)(2,1)S(1)}, bf16[4096,128]{1,0:T(8,128)(2,1)}, u32[]{:S(2)}) copy-start(bf16[4096,128]{1,0:T(8,128)(2,1)} %param.8) | copy-start | bytes 3145732
  91.7 35.6 %all-to-all-start.5 = ((bf16[16,256,128]{2,1,0:T(8,128)(2,1)}), bf16[16,256,128]{2,1,0:T(8,128)(2,1)}, u32[]{:S(2)}, u32[]{:S(2)}) async-start(bf16[16,256,128]{2,1,0:T(8,128)(2,1)} %bitcast.156), calls=%async_computation.5 | async-start | bytes 2097152 | tf_op jit(solution)/shard_map/all_to_all | solution.py:27
  96.2 2.6 copy-start.10
  96.2 2.8 copy-start.11
  96.2 2.8 copy-start.12
  101.6 1.0 copy-start.3
  127.3 33.1 %all-to-all-start.3 = ((bf16[16,256,128]{1,2,0:T(8,128)(2,1)}), bf16[16,256,128]{1,2,0:T(8,128)(2,1)}, u32[]{:S(2)}, u32[]{:S(2)}) async-start(bf16[16,256,128]{1,2,0:T(8,128)(2,1)} %copy.76), calls=%async_computation.3 | async-start | bytes 2097152 | tf_op jit(solution)/shard_map/all_to_all | solution.py:27
  168.5 35.2 %copy-start.7 = (bf16[8,512,128]{2,0,1:T(8,128)(2,1)S(1)}, bf16[8,512,128]{2,0,1:T(8,128)(2,1)}, u32[]{:S(2)}) copy-start(bf16[8,512,128]{2,0,1:T(8,128)(2,1)} %copy.81) | copy-start | bytes 3145732
  240.8 20.2 %all-to-all-start.10 = ((bf16[8,512,128]{2,1,0:T(8,128)(2,1)}), bf16[8,512,128]{2,1,0:T(8,128)(2,1)}, u32[]{:S(2)}, u32[]{:S(2)}) async-start(bf16[8,512,128]{2,1,0:T(8,128)(2,1)} %bitcast.147), calls=%async_computation.10 | async-start | bytes 2097152 | tf_op jit(solution)/shard_map/all_to_all | solution.py:27
  261.0 30.5 %all-to-all-start.8 = ((bf16[16,32,8,128]{3,2,1,0:T(8,128)(2,1)}), bf16[16,32,8,128]{3,2,1,0:T(8,128)(2,1)S(1)}, u32[]{:S(2)}, u32[]{:S(2)}) async-start(bf16[16,32,8,128]{3,2,1,0:T(8,128)(2,1)} %bitcast.159), calls=%async_computation.8 | async-start | bytes 2097152 | tf_op jit(solution)/shard_map/all_to_all | solution.py:27
  291.5 5.5 %copy-start.5 = (bf16[16,32,8,128]{3,2,1,0:T(8,128)(2,1)}, bf16[16,32,8,128]{3,2,1,0:T(8,128)(2,1)S(1)}, u32[]{:S(2)}) copy-start(bf16[16,32,8,128]{3,2,1,0:T(8,128)(2,1)S(1)} %all-to-all-done.8) | copy-start | bytes 3145732
  291.5 35.6 %all-to-all-start.4 = ((bf16[16,256,128]{1,2,0:T(8,128)(2,1)}), bf16[16,256,128]{1,2,0:T(8,128)(2,1)}, u32[]{:S(2)}, u32[]{:S(2)}) async-start(bf16[16,256,128]{1,2,0:T(8,128)(2,1)} %fusion.59), calls=%async_computation.4 | async-start | bytes 2097152 | tf_op jit(solution)/shard_map/all_to_all | solution.py:27
  327.1 20.2 %all-to-all-start.9 = ((bf16[8,512,128]{2,1,0:T(8,128)(2,1)}), bf16[8,512,128]{2,1,0:T(8,128)(2,1)}, u32[]{:S(2)}, u32[]{:S(2)}) async-start(bf16[8,512,128]{2,1,0:T(8,128)(2,1)} %bitcast.158), calls=%async_computation.9 | async-start | bytes 2097152 | tf_op jit(solution)/shard_map/all_to_all | solution.py:27
  347.3 19.4 %all-to-all-start.12 = ((bf16[8,2,32,8,128]{4,3,1,2,0:T(8,128)(2,1)}), bf16[8,2,32,8,128]{4,3,1,2,0:T(8,128)(2,1)S(1)}, u32[]{:S(2)}, u32[]{:S(2)}) async-start(bf16[8,2,32,8,128]{4,3,1,2,0:T(8,128)(2,1)} %bitcast.143), calls=%async_computation.12 | async-start | bytes 2097152 | tf_op jit(solution)/shard_map/all_to_all | solution.py:27
  350.9 2.7 copy-start.4
  361.9 1.4 copy-start.8
  362.7 25.2 %copy-start.6 = (bf16[16,32,8,128]{3,2,1,0:T(8,128)(2,1)S(1)}, bf16[16,32,8,128]{3,2,1,0:T(8,128)(2,1)}, u32[]{:S(2)}) copy-start(bf16[16,32,8,128]{3,2,1,0:T(8,128)(2,1)} %copy-done.5) | copy-start | bytes 3145732
  362.7 18.1 %collective-permute-start = (bf16[8,32,512]{2,1,0:T(8,128)(2,1)}, bf16[8,32,512]{2,1,0:T(8,128)(2,1)S(1)}, u32[]{:S(2)}, u32[]{:S(2)}) collective-permute-start(bf16[8,32,512]{2,1,0:T(8,128)(2,1)} %fusion.105), channel_id=1, source_target_pairs={{0,8},{8,0},{1,9},{9,1},{2,10},{10,2},{3,11},{11,3},{4,12},{12,4},... | collective-permute-start | bytes 786440 | tf_op jit(solution)/shard_map/ppermute | solution.py:123
  366.9 20.3 %collective-permute-start.1 = (f32[32,8,128]{2,1,0:T(8,128)S(1)}, f32[32,8,128]{2,1,0:T(8,128)S(1)}, u32[]{:S(2)}, u32[]{:S(2)}) collective-permute-start(f32[32,8,128]{2,1,0:T(8,128)S(1)} %dynamic-slice_bitcast_fusion), channel_id=1, source_target_pairs={{0,8},{8,0},{1,9},{9,1},{2,10},{10,2},{3,11},{11,3},{4,12},{12,4},... | collective-permute-start | bytes 393224 | tf_op jit(solution)/shard_map/ppermute | solution.py:116
  382.7 14.9 %all-to-all-start.11 = ((f32[8,32,512]{2,1,0:T(8,128)}), f32[8,32,512]{2,1,0:T(8,128)}, u32[]{:S(2)}, u32[]{:S(2)}) async-start(f32[8,32,512]{2,1,0:T(8,128)} %bitcast_add_fusion.2), calls=%async_computation.11 | async-start | bytes 1048576 | tf_op jit(solution)/shard_map/all_to_all | solution.py:27
  387.9 11.6 %copy-start.1 = (bf16[32,128,128]{2,1,0:T(8,128)(2,1)S(1)}, bf16[32,128,128]{2,1,0:T(8,128)(2,1)}, u32[]{:S(2)}) copy-start(bf16[32,128,128]{2,1,0:T(8,128)(2,1)} %param.11) | copy-start | bytes 3145732
